TPU v7x, 32 devices: a whole 2x2x4 slice. The times are simulated.
32 devices in a mesh: dp: 4 (over y, core), expert: 8 (over z, x).
Axes of the slice: x: 2, y: 2, z: 4, core: 2. Of those that a mesh axis runs over, the one named last changes fastest.
Arguments:
- tokens: bfloat16 [4, 1024, 4096], P('dp', 'expert'), may hold values from -20 to 20
- router_weight: bfloat16 [4096, 128], replicated
- chosen: int32 [4, 1, 128], P('dp'), may hold values from 0 to 1023, as said below
- w_gate: bfloat16 [4096, 1536], P(None, 'expert'), may hold values from -0.09375 to 0.09375
- w_up: bfloat16 [4096, 1536], P(None, 'expert'), may hold values from -0.09375 to 0.09375
- w_down: bfloat16 [1536, 4096], P('expert'), may hold values from -0.15625 to 0.15625
Outputs:
- combined: bfloat16 [4, 1024, 4096], P('dp', 'expert')
- z_loss: float32 [], replicated
Inputs may be any that keep to these rules, and one draw needn't show every extreme that they name: Each list chosen[g, e] holds 128 distinct positions of window g; at most 32 of them lie in any one aligned block of 128 positions (the tokens of one device), and some block holds exactly 32.
All inputs are finite; a program needn't handle non-finite values.
Results may differ from a plain program's by a relative error of at most 0.009.
Values may be sent and summed in bfloat16 or wider, within the bound.
A program may use at most 64 MiB of HBM per device.

v0:
```python
import jax
import jax.numpy as jnp
from jax import lax
from jax.sharding import PartitionSpec as P


def partner(value, axis, stride):
    mask = 2**stride
    pairs = [(source, source ^ mask) for source in range(lax.axis_size(axis))]
    return lax.ppermute(value, axis, pairs)


def block_index(device, bit_list):
    levels = len(bit_list)
    block_sum = jnp.zeros_like(device)
    for position, bit_no in enumerate(bit_list):
        block_sum = block_sum + (device >> bit_no & 1) * (1 << levels - 1 - position)
    return block_sum


def body(tokens, router_weight, chosen, w_gate, w_up, w_down):
    token_rows = tokens[0]
    picked = chosen[0]
    experts_here = picked.shape[0]
    rows_dev = token_rows.shape[0]
    width = token_rows.shape[1]
    devices = lax.axis_size("expert")
    split = devices // experts_here
    levels = split.bit_length() - 1
    most = 2 * picked.shape[1] // devices
    piece_width = width // split
    my_index = lax.axis_index("expert")
    bit_list = list(range(levels))
    logits = jnp.dot(token_rows, router_weight, preferred_element_type=jnp.float32)
    highest = jnp.max(logits, axis=1, keepdims=True)
    log_total = highest[:, 0] + jnp.log(jnp.sum(jnp.exp(logits - highest), axis=1))
    loss_total = lax.psum(jnp.sum(log_total * log_total), ("dp", "expert"))
    z_loss = loss_total / (lax.axis_size("dp") * devices * rows_dev)
    local_pos = picked - my_index * rows_dev
    inside = (local_pos >= 0) & (local_pos < rows_dev)
    inside_int = inside.astype(jnp.int32)
    rank = jnp.cumsum(inside_int, axis=1) - inside_int
    slot = jnp.where(inside, rank, most)
    expert_ids = jnp.arange(experts_here, dtype=jnp.int32)[:, None]
    slot_token = (
        jnp.full((experts_here, most), rows_dev, jnp.int32)
        .at[expert_ids, slot]
        .set(local_pos, mode="drop")
    )
    member = jnp.any(
        local_pos[:, :, None] == jnp.arange(rows_dev, dtype=jnp.int32)[None, None, :], axis=1
    ).T
    window = logits[:, :experts_here]
    peak = jnp.max(jnp.where(member, window, -1e30), axis=1, keepdims=True)
    peak = jnp.where(jnp.any(member, axis=1, keepdims=True), peak, 0.0)
    raised = jnp.where(member, jnp.exp(jnp.where(member, window - peak, -60.0)), 0.0)
    denom = jnp.sum(raised, axis=1, keepdims=True)
    combine = raised / jnp.where(denom > 0, denom, 1.0)
    combine_pad = jnp.concatenate([combine, jnp.zeros((1, experts_here), jnp.float32)], axis=0)
    slot_weight = combine_pad[slot_token, expert_ids]
    rows_pad = jnp.concatenate([token_rows, jnp.zeros((1, width), token_rows.dtype)], axis=0)
    slot_rows = rows_pad[slot_token]
    device_ids = jnp.arange(split, dtype=jnp.int32)
    blocks = block_index(device_ids, bit_list)
    inverse = jnp.argsort(blocks)
    outgoing = jnp.repeat(slot_rows, split, axis=0)
    arrived = lax.all_to_all(outgoing, "expert", split_axis=0, concat_axis=0, tiled=True)
    flat_rows = arrived.reshape(devices * most, width)
    gate = jnp.dot(flat_rows, w_gate, preferred_element_type=jnp.float32)
    upper = jnp.dot(flat_rows, w_up, preferred_element_type=jnp.float32)
    hidden = (jax.nn.silu(gate) * upper).astype(jnp.bfloat16)
    rounded = (
        jnp.dot(hidden, w_down, preferred_element_type=jnp.float32)
        .astype(jnp.bfloat16)
        .reshape(devices, most, width)
    )
    held = rounded.reshape(devices, most, 1, width)
    for bit_no in bit_list:
        half_width = held.shape[3] // 2
        lower_half = held[:, :, :, :half_width]
        upper_half = held[:, :, :, half_width:]
        lower_side = my_index >> bit_no & 1 == 0
        keeping = jnp.where(lower_side, lower_half, upper_half)
        sending = jnp.where(lower_side, upper_half, lower_half)
        received = partner(sending, "expert", bit_no)
        held = jnp.concatenate([keeping, received], axis=2)
    expert_out = jnp.sum(held.astype(jnp.float32), axis=2).astype(jnp.bfloat16)
    returned = lax.all_to_all(expert_out, "expert", split_axis=0, concat_axis=0, tiled=True)
    returned = jnp.take(returned.reshape(experts_here, split, most, piece_width), inverse, axis=1)
    full_out = returned.transpose(0, 2, 1, 3).reshape(experts_here, most, width)
    contrib = slot_weight[:, :, None] * full_out.astype(jnp.float32)
    mixed = (
        jnp.zeros((rows_dev, width), jnp.float32)
        .at[slot_token.reshape(-1)]
        .add(contrib.reshape(-1, width), mode="drop")
    )
    return (mixed.astype(jnp.bfloat16)[None], z_loss)


def solution(mesh):
    in_specs = (
        P("dp", "expert", None),
        P(),
        P("dp", None, None),
        P(None, "expert"),
        P(None, "expert"),
        P("expert", None),
    )
    out_specs = (P("dp", "expert", None), P())
    return jax.shard_map(body, mesh=mesh, in_specs=in_specs, out_specs=out_specs, check_vma=False)
```

profile of v0, /device:TPU:0, one launch (start us, length us, event | category | flops | bytes accessed | tf_op | source)
XLA Modules:
  0.0 232.6 jit_solution(9588220514075788087)
XLA Ops:
  0.6 0.0 copy-start
  0.6 0.8 and_bitcast_fusion
  1.4 0.7 subtract_bitcast_fusion
  2.1 0.1 copy.16
  2.2 0.2 reduce_window_sum.11
  2.4 0.1 pad_bitcast_fusion
  2.5 0.2 fusion.13
  2.7 1.0 scatter_custom_fusion
  3.7 1.3 concatenate.22
  5.0 0.7 gather_fusion.1
  5.8 1.5 reshape.214
  7.3 7.3 %all-to-all-start = ((bf16[8,32,4096]{2,1,0:T(8,128)(2,1)}), bf16[8,32,4096]{2,1,0:T(8,128)(2,1)}, u32[]{:S(2)}, u32[]{:S(2)}) async-start(bf16[8,32,4096]{2,1,0:T(8,128)(2,1)} %reshape.214), calls=%async_computation | async-start | bytes 4194304 | tf_op jit(solution)/shard_map/all_to_all | solution.py:67
  14.6 0.0 copy-start.2
  14.6 48.3 %all-to-all-done = bf16[8,32,4096]{2,1,0:T(8,128)(2,1)} async-done(((bf16[8,32,4096]{2,1,0:T(8,128)(2,1)}), bf16[8,32,4096]{2,1,0:T(8,128)(2,1)}, u32[]{:S(2)}, u32[]{:S(2)}) %all-to-all-start) | async-done | bytes 2097184 | tf_op jit(solution)/shard_map/all_to_all | solution.py:67
  62.9 2.9 %fusion.34 = f32[256,192]{0,1:T(8,128)S(1)} fusion(bf16[256,4096]{1,0:T(8,128)(2,1)} %bitcast.12, bf16[4096,192]{0,1:T(8,128)(2,1)} %param.9), kind=kOutput, calls=%fused_computation.82 | convolution fusion | flops 402653184 | bytes 3866624 | tf_op jit(solution)/shard_map/dot_general | solution.py:69
  65.8 0.0 copy-done
  65.8 0.0 copy-done.2
  65.8 5.4 %convolution_convert_fusion = bf16[256,4096]{1,0:T(8,128)(2,1)} fusion(bf16[192,4096]{1,0:T(8,128)(2,1)S(1)} %copy-done, bf16[256,4096]{1,0:T(8,128)(2,1)} %bitcast.12, bf16[4096,192]{0,1:T(8,128)(2,1)S(1)} %copy-done.2, f32[256,192]{0,1:T(8,128)S(1)} %fusion.34), kind=kOutput, calls=%fused_computation.5 | convolution fusion | flops 806649856 | bytes 7536640 | tf_op jit(solution)/shard_map/dot_general | solution.py:73
  71.3 2.6 %broadcast_select_fusion.1 = (bf16[8,32,1,2048]{3,1,0,2:T(8,128)(2,1)S(1)}, bf16[8,32,1,2048]{3,1,0,2:T(8,128)(2,1)}) fusion(pred[]{:T(512)S(6)} %eq.35, bf16[8,32,1,4096]{3,1,0,2:T(8,128)(2,1)} %bitcast.69), kind=kLoop, calls=%fused_computation.21 | loop fusion | flops 1048576 | bytes 4194305 | tf_op jit(solution)/shard_map/jit(_where)/select_n | solution.py:83
  73.9 1.5 collective-permute-start
  75.4 22.7 %collective-permute-done = bf16[8,32,1,2048]{3,1,0,2:T(8,128)(2,1)} collective-permute-done((bf16[8,32,1,2048]{3,1,0,2:T(8,128)(2,1)}, bf16[8,32,1,2048]{3,1,0,2:T(8,128)(2,1)}, u32[]{:S(2)}, u32[]{:S(2)}) %collective-permute-start) | collective-permute-done | bytes 1048608 | tf_op jit(solution)/shard_map/ppermute | solution.py:10
  98.1 3.4 %broadcast_select_fusion.3 = (bf16[8,32,2,1024]{3,1,0,2:T(8,128)(2,1)}, bf16[8,32,2,1024]{3,1,0,2:T(8,128)(2,1)}) fusion(pred[]{:T(512)S(6)} %eq.34, bf16[8,32,1,2048]{3,1,0,2:T(8,128)(2,1)} %collective-permute-done, bf16[8,32,1,2048]{3,1,0,2:T(8,128)(2,1)S(1)} %get-tuple-element.8), kind=kLoop, calls=%fused_computation.23 | loop fusion | flops 7340032 | bytes 4194305 | tf_op jit(solution)/shard_map/jit(_where)/select_n | solution.py:83
  101.5 0.0 copy-start.1
  101.5 0.6 collective-permute-start.1
  102.2 1.0 sort.17
  103.2 0.0 copy-start.3
  103.2 21.8 %collective-permute-done.1 = bf16[8,32,2,1024]{3,1,0,2:T(8,128)(2,1)} collective-permute-done((bf16[8,32,2,1024]{3,1,0,2:T(8,128)(2,1)}, bf16[8,32,2,1024]{3,1,0,2:T(8,128)(2,1)}, u32[]{:S(2)}, u32[]{:S(2)}) %collective-permute-start.1) | collective-permute-done | bytes 1048608 | tf_op jit(solution)/shard_map/ppermute | solution.py:10
  125.0 2.6 %broadcast_select_fusion.4 = (bf16[8,32,4,512]{3,1,0,2:T(8,128)(2,1)S(1)}, bf16[8,32,512]{2,1,0:T(8,128)(2,1)S(1)}) fusion(pred[]{:T(512)S(6)} %eq.33, bf16[8,32,2,1024]{3,1,0,2:T(8,128)(2,1)} %collective-permute-done.1, bf16[8,32,2,1024]{3,1,0,2:T(8,128)(2,1)} %get-tuple-element.6), kind=kLoop, calls=%fused_computation.24 | loop fusion | flops 7733248 | bytes 3407873 | tf_op jit(solution)/shard_map/jit(_where)/select_n | solution.py:84
  127.6 3.4 %collective-permute-start.2 = (bf16[8,32,4,512]{3,1,0,2:T(8,128)(2,1)S(1)}, bf16[8,32,4,512]{3,1,0,2:T(8,128)(2,1)}, u32[]{:S(2)}, u32[]{:S(2)}) collective-permute-start(bf16[8,32,4,512]{3,1,0,2:T(8,128)(2,1)S(1)} %get-tuple-element.4), channel_id=1, source_target_pairs={{0,4},{1,5},{2,6},{3,7},{4,0},{5,1},{6,2},{7,3},{8,12},{9,13},{10,... | collective-permute-start | bytes 3145736 | tf_op jit(solution)/shard_map/ppermute | solution.py:10
  131.0 0.0 copy-done.1
  131.0 0.0 copy-done.3
  131.0 0.6 fusion.32
  131.6 0.6 multiply_reduce_fusion
  132.3 0.1 fusion.14
  132.4 43.1 %collective-permute-done.2 = bf16[8,32,4,512]{3,1,0,2:T(8,128)(2,1)} collective-permute-done((bf16[8,32,4,512]{3,1,0,2:T(8,128)(2,1)S(1)}, bf16[8,32,4,512]{3,1,0,2:T(8,128)(2,1)}, u32[]{:S(2)}, u32[]{:S(2)}) %collective-permute-start.2) | collective-permute-done | bytes 1048608 | tf_op jit(solution)/shard_map/ppermute | solution.py:10
  175.5 1.4 reduce_sum.43
  176.9 0.8 reduce_sum.44
  177.7 4.9 %all-to-all-start.1 = ((bf16[8,32,512]{2,1,0:T(8,128)(2,1)}), bf16[8,32,512]{2,1,0:T(8,128)(2,1)S(1)}, u32[]{:S(2)}, u32[]{:S(2)}) async-start(bf16[8,32,512]{2,1,0:T(8,128)(2,1)} %reduce_sum.44), calls=%async_computation.1 | async-start | bytes 524288 | tf_op jit(solution)/shard_map/all_to_all | solution.py:88
  182.6 41.2 %psum.7 = f32[]{:T(128)} all-reduce(f32[]{:T(128)} %multiply_reduce_fusion), channel_id=1, replica_groups=mesh['dp'=4,'expert'=8] {'dp','expert'}, use_global_device_ids=true, to_apply=%region_10.11 | all-reduce | flops 1 | bytes 8 | tf_op jit(solution)/shard_map/psum | solution.py:37
  223.8 0.7 gather_fusion
  225.2 0.0 all-to-all-done.1
  225.2 0.6 gather_fusion.2
  225.8 0.1 fusion.33
  225.9 2.8 %scatter_custom_fusion.1 = f32[128,4096]{1,0:T(8,128)} fusion(s32[32]{0:T(128)S(1)} %fusion.24, f32[]{:T(128)} %constant.20.clone.1, f32[32,4096]{1,0:T(8,128)S(1)} %bitcast.71, f32[32]{0:T(128)S(1)} %gather_fusion), kind=kCustom, calls=%fused_computation.18 | custom fusion | flops 262144 | bytes 2621956 | tf_op jit(solution)/shard_map/scatter-add | solution.py:95
  228.7 2.7 %convert_bitcast_fusion = bf16[1,128,4096]{2,1,0:T(8,128)(2,1)} fusion(f32[128,4096]{1,0:T(8,128)} %scatter_custom_fusion.1), kind=kLoop, calls=%fused_computation.16 | loop fusion | flops 524288 | bytes 3145728 | tf_op jit(solution)/shard_map/broadcast_in_dim | solution.py:97
  (16 shorter events, 0.2 us)
Async XLA Ops:
  0.6 65.2 %copy-start = (bf16[192,4096]{1,0:T(8,128)(2,1)S(1)}, bf16[192,4096]{1,0:T(8,128)(2,1)}, u32[]{:S(2)}) copy-start(bf16[192,4096]{1,0:T(8,128)(2,1)} %param.11) | copy-start | bytes 4718596
  7.3 55.6 %all-to-all-start = ((bf16[8,32,4096]{2,1,0:T(8,128)(2,1)}), bf16[8,32,4096]{2,1,0:T(8,128)(2,1)}, u32[]{:S(2)}, u32[]{:S(2)}) async-start(bf16[8,32,4096]{2,1,0:T(8,128)(2,1)} %reshape.214), calls=%async_computation | async-start | bytes 4194304 | tf_op jit(solution)/shard_map/all_to_all | solution.py:67
  14.6 51.2 %copy-start.2 = (bf16[4096,192]{0,1:T(8,128)(2,1)S(1)}, bf16[4096,192]{0,1:T(8,128)(2,1)}, u32[]{:S(2)}) copy-start(bf16[4096,192]{0,1:T(8,128)(2,1)} %param.10) | copy-start | bytes 4718596
  73.9 24.2 %collective-permute-start = (bf16[8,32,1,2048]{3,1,0,2:T(8,128)(2,1)}, bf16[8,32,1,2048]{3,1,0,2:T(8,128)(2,1)}, u32[]{:S(2)}, u32[]{:S(2)}) collective-permute-start(bf16[8,32,1,2048]{3,1,0,2:T(8,128)(2,1)} %get-tuple-element.9), channel_id=1, source_target_pairs={{0,1},{1,0},{2,3},{3,2},{4,5},{5,4},{6,7},{7,6},{8,9},{9,8},{10,11... | collective-permute-start | bytes 3145736 | tf_op jit(solution)/shard_map/ppermute | solution.py:10
  101.5 29.5 %copy-start.1 = (bf16[1,128,4096]{2,1,0:T(8,128)(2,1)S(1)}, bf16[1,128,4096]{2,1,0:T(8,128)(2,1)}, u32[]{:S(2)}) copy-start(bf16[1,128,4096]{2,1,0:T(8,128)(2,1)} %param.6) | copy-start | bytes 3145732
  101.5 23.4 %collective-permute-start.1 = (bf16[8,32,2,1024]{3,1,0,2:T(8,128)(2,1)}, bf16[8,32,2,1024]{3,1,0,2:T(8,128)(2,1)}, u32[]{:S(2)}, u32[]{:S(2)}) collective-permute-start(bf16[8,32,2,1024]{3,1,0,2:T(8,128)(2,1)} %get-tuple-element.7), channel_id=1, source_target_pairs={{0,2},{1,3},{2,0},{3,1},{4,6},{5,7},{6,4},{7,5},{8,10},{9,11},{10,... | collective-permute-start | bytes 3145736 | tf_op jit(solution)/shard_map/ppermute | solution.py:10
  103.2 27.9 %copy-start.3 = (bf16[4096,128]{1,0:T(8,128)(2,1)S(1)}, bf16[4096,128]{1,0:T(8,128)(2,1)}, u32[]{:S(2)}) copy-start(bf16[4096,128]{1,0:T(8,128)(2,1)} %param.7) | copy-start | bytes 3145732
  127.6 47.9 %collective-permute-start.2 = (bf16[8,32,4,512]{3,1,0,2:T(8,128)(2,1)S(1)}, bf16[8,32,4,512]{3,1,0,2:T(8,128)(2,1)}, u32[]{:S(2)}, u32[]{:S(2)}) collective-permute-start(bf16[8,32,4,512]{3,1,0,2:T(8,128)(2,1)S(1)} %get-tuple-element.4), channel_id=1, source_target_pairs={{0,4},{1,5},{2,6},{3,7},{4,0},{5,1},{6,2},{7,3},{8,12},{9,13},{10,... | collective-permute-start | bytes 3145736 | tf_op jit(solution)/shard_map/ppermute | solution.py:10
  177.7 47.5 %all-to-all-start.1 = ((bf16[8,32,512]{2,1,0:T(8,128)(2,1)}), bf16[8,32,512]{2,1,0:T(8,128)(2,1)S(1)}, u32[]{:S(2)}, u32[]{:S(2)}) async-start(bf16[8,32,512]{2,1,0:T(8,128)(2,1)} %reduce_sum.44), calls=%async_computation.1 | async-start | bytes 524288 | tf_op jit(solution)/shard_map/all_to_all | solution.py:88
where the time goes:
time: 233 us
  waiting for transfers between devices  136 us (58%)
  blocking collectives  41.2 us (18%)
  other arithmetic  20 us (9%)
  starting transfers between devices  17.7 us (8%)
  matrix products  8.87 us (4%)
  local copies, waits for them, and re-layouts  6.09 us (3%)
  between operations  2.61 us (1%)
    ppermute x3, waiting for transfers between devices, partner(): return lax.ppermute(value, axis, pairs)  87.7 us
    all_to_all x1, waiting for transfers between devices, body(): lax.all_to_all(outgoing, 'expert', split_axis=0, concat_axis=0, tiled=True)  48.3 us
    psum x1, blocking collectives, body(): loss_total = lax.psum(jnp.sum(log_total * log_total), ('dp', 'expert'))  41.2 us
    all_to_all x1, starting transfers between devices, body(): lax.all_to_all(outgoing, 'expert', split_axis=0, concat_axis=0, tiled=True)  7.28 us
    select_n x2, other arithmetic, body(): keeping = jnp.where(lower_side, lower_half, upper_half)  6.07 us
    ppermute x3, starting transfers between devices, partner(): return lax.ppermute(value, axis, pairs)  5.55 us
    dot_general x1, matrix products, body(): jnp.dot(hidden, w_down, preferred_element_type=jnp.float32)  5.43 us
    all_to_all x1, starting transfers between devices, body(): lax.all_to_all(expert_out, 'expert', split_axis=0, concat_axis=0, tiled=T...  4.91 us
  transfers between devices with their start and end apart: 5, of which 4 were waited for; matrix products, arithmetic and copies ran while one was open for 1% of the time, Pallas kernels for 0%

commit v1 on v0

v1 whole, which is shorter than its diff:
```python
import functools

import jax
import jax.numpy as jnp
from jax import lax
from jax.experimental import pallas as pl
from jax.experimental.pallas import tpu as pltpu
from jax.sharding import PartitionSpec as P

MESH = pl.DeviceIdType.MESH
F32 = jnp.float32
BF16 = jnp.bfloat16


def flip(index, mask):
    result = index
    bit = 0
    while mask >> bit:
        if mask >> bit & 1:
            result = result + 2**bit * (1 - 2 * (index // 2**bit % 2))
        bit += 1
    return result


class Tree:
    def __init__(self, levels, order):
        self.blocks = 2**levels
        self.bit = {}
        for j in range(1, self.blocks):
            self.bit[j] = [b for b in order if j >> b & 1][-1]
        self.parent = {j: j ^ 1 << b for j, b in self.bit.items()}
        self.children = [
            sorted((j for j in self.parent if self.parent[j] == i), key=lambda j: order.index(self.bit[j]))
            for i in range(self.blocks)
        ]
        self.depth = [bin(j).count("1") for j in range(self.blocks)]
        self.height = [self._height(j) for j in range(self.blocks)]

    def _height(self, j):
        return 1 + max(self._height(i) for i in self.children[j]) if self.children[j] else 0


def kernel(cfg, *refs):
    groups, split, most, dp_bits, ex_bits, trees, chunk, tokens_all = cfg
    (tok_h, rw_h, chosen_ref, wg_h, wu_h, wd_h, out_ref, z_ref,
     tok, rw, wg, wu, wd, rows_x, send_y, recv_y, part_y, z_acc, z_in,
     local_sem, ag_send, ag_recv, rs_send, rs_recv, z_send, z_recv) = refs[:26]
    levels = split.bit_length() - 1
    me = lax.axis_index("expert")
    me_dp = lax.axis_index("dp")
    my_group = me // split
    rows_dev, width = tok.shape
    cap = chosen_ref.shape[1]
    block = groups * most
    chunks = len(trees)

    local = [
        pltpu.make_async_copy(src, dst, local_sem.at[i])
        for i, (src, dst) in enumerate(((tok_h, tok), (wg_h, wg), (wu_h, wu), (rw_h, rw), (wd_h, wd)))
    ]
    for copy in local:
        copy.start()

    ex_masks = [1 << b for b in range(levels)] + [split * k for k in range(1, groups)]
    partners = [{"expert": flip(me, mask)} for mask in ex_masks]
    partners += [{"dp": flip(me_dp, 1 << b)} for b in range(dp_bits)]
    barrier = pltpu.get_barrier_semaphore()
    for partner in partners:
        pl.semaphore_signal(barrier, inc=1, device_id=partner, device_id_type=MESH)

    t_sub = lax.broadcasted_iota(jnp.int32, (rows_dev, cap), 0)
    sq_row = lax.broadcasted_iota(jnp.int32, (rows_dev, rows_dev), 0)
    sq_col = lax.broadcasted_iota(jnp.int32, (rows_dev, rows_dev), 1)
    before = (sq_row < sq_col).astype(F32).astype(BF16)
    after = (sq_col < sq_row).astype(F32).astype(BF16)
    slot_sub = lax.broadcasted_iota(jnp.int32, (most, rows_dev), 0).astype(F32)
    slot_lane = lax.broadcasted_iota(jnp.int32, (rows_dev, most), 1).astype(F32)
    picks, places, members = [], [], []
    for k in range(groups):
        row = chosen_ref[pl.ds(flip(my_group, k), 1), :] - me * rows_dev
        equal = (row == t_sub).astype(F32)
        member = jnp.max(equal, axis=1, keepdims=True)
        ones = jnp.ones((8, cap), BF16)
        member_row = lax.dot_general(ones, equal.astype(BF16), (((1,), (1,)), ((), ())), preferred_element_type=F32)
        rank_row = jnp.dot(member_row.astype(BF16), before, preferred_element_type=F32)
        pick = jnp.where(member_row[0:1] > 0.5, (rank_row[0:1] == slot_sub).astype(F32), 0.0)
        wide = jnp.broadcast_to(member, (rows_dev, most))
        rank_col = jnp.dot(after, wide.astype(BF16), preferred_element_type=F32)
        place = jnp.where(wide > 0.5, (rank_col == slot_lane).astype(F32), 0.0)
        picks.append(pick.astype(BF16))
        places.append(place.astype(BF16))
        members.append(member)

    def cols(c):
        return pl.ds(c * chunk, chunk)

    def ag_copy(c, j):
        tree = trees[c]
        return pltpu.make_async_remote_copy(
            src_ref=rows_x.at[tree.parent[j], :, cols(c)],
            dst_ref=rows_x.at[j, :, cols(c)],
            send_sem=ag_send.at[c, j],
            recv_sem=ag_recv.at[c, j],
            device_id={"expert": flip(me, 1 << tree.bit[j])},
            device_id_type=MESH,
        )

    def rs_copy(c, j):
        tree = trees[c]
        return pltpu.make_async_remote_copy(
            src_ref=send_y.at[j, :, cols(c)],
            dst_ref=recv_y.at[j, :, cols(c)],
            send_sem=rs_send.at[c, j],
            recv_sem=rs_recv.at[c, j],
            device_id={"expert": flip(me, 1 << tree.bit[j])},
            device_id_type=MESH,
        )

    z_steps = [("expert", flip(me, 1 << b)) for b in range(ex_bits)]
    z_steps += [("dp", flip(me_dp, 1 << b)) for b in range(dp_bits)]

    def z_copy(s):
        axis, partner = z_steps[s]
        return pltpu.make_async_remote_copy(
            src_ref=z_acc.at[s],
            dst_ref=z_in.at[s],
            send_sem=z_send.at[s],
            recv_sem=z_recv.at[s],
            device_id={axis: partner},
            device_id_type=MESH,
        )

    def z_advance(s):
        if s > 0:
            z_copy(s - 1).wait()
            z_acc[s] = z_acc[s - 1] + z_in[s - 1]
        if s < len(z_steps):
            z_copy(s).start()

    pl.semaphore_wait(barrier, len(partners))
    local[0].wait()
    if groups == 1:
        for c in range(chunks):
            rows_x[0, :, cols(c)] = jnp.dot(picks[0], tok[:, cols(c)], preferred_element_type=F32).astype(BF16)
            for j in trees[c].children[0]:
                ag_copy(c, j).start()
    else:
        slots, stage, back_out, back_in, ex_send, ex_recv, bk_send, bk_recv = refs[26:]

        def across(k, src, dst, send, recv):
            return pltpu.make_async_remote_copy(
                src_ref=src.at[k],
                dst_ref=dst.at[k],
                send_sem=send.at[k],
                recv_sem=recv.at[k],
                device_id={"expert": flip(me, split * k)},
                device_id_type=MESH,
            )

        def spread(k):
            sub = lax.broadcasted_iota(jnp.int32, (block, most), 0)
            lane = lax.broadcasted_iota(jnp.int32, (block, most), 1)
            return (sub == lane + k * most).astype(F32).astype(BF16)

        def collect(k):
            sub = lax.broadcasted_iota(jnp.int32, (most, block), 0)
            lane = lax.broadcasted_iota(jnp.int32, (most, block), 1)
            return (lane == sub + k * most).astype(F32).astype(BF16)

        for k in range(groups):
            for c in range(chunks):
                slots[k, :, cols(c)] = jnp.dot(picks[k], tok[:, cols(c)], preferred_element_type=F32).astype(BF16)
            if k:
                across(k, slots, stage, ex_send, ex_recv).start()
        for k in range(1, groups):
            across(k, slots, stage, ex_send, ex_recv).wait()
        for c in range(chunks):
            total = jnp.dot(spread(0), slots[0, :, cols(c)], preferred_element_type=F32)
            for k in range(1, groups):
                total = total + jnp.dot(spread(k), stage[k, :, cols(c)], preferred_element_type=F32)
            rows_x[0, :, cols(c)] = total.astype(BF16)
            for j in trees[c].children[0]:
                ag_copy(c, j).start()

    local[3].wait()
    logits = jnp.dot(tok[...], rw[...], preferred_element_type=F32)
    highest = jnp.max(logits, axis=1, keepdims=True)
    log_total = highest + jnp.log(jnp.sum(jnp.exp(logits - highest), axis=1, keepdims=True))
    z_part = jnp.sum(log_total * log_total, axis=0, keepdims=True)
    z_acc[0] = jnp.broadcast_to(z_part, z_acc.shape[1:])
    lane = lax.broadcasted_iota(jnp.int32, logits.shape, 1)
    window = [
        jnp.sum(jnp.where(lane == flip(my_group, k), logits, 0.0), axis=1, keepdims=True) for k in range(groups)
    ]
    peak = jnp.where(members[0] > 0.5, window[0], -1e30)
    some = members[0]
    for k in range(1, groups):
        peak = jnp.maximum(peak, jnp.where(members[k] > 0.5, window[k], -1e30))
        some = jnp.maximum(some, members[k])
    peak = jnp.where(some > 0.5, peak, 0.0)
    raised = [
        jnp.where(members[k] > 0.5, jnp.exp(jnp.where(members[k] > 0.5, window[k] - peak, -60.0)), 0.0)
        for k in range(groups)
    ]
    denom = functools.reduce(lambda a, b: a + b, raised)
    weights = [value / jnp.where(denom > 0, denom, 1.0) for value in raised]

    local[1].wait()
    local[2].wait()
    gate = jnp.zeros((split * block, wg.shape[1]), F32)
    upper = jnp.zeros((split * block, wg.shape[1]), F32)
    z_done = 0
    for t in range(chunks + levels - 1):
        for depth in range(levels, 0, -1):
            c = t - (depth - 1)
            if 0 <= c < chunks:
                for j in range(split):
                    if trees[c].depth[j] == depth:
                        ag_copy(c, j).wait_recv()
                        for i in trees[c].children[j]:
                            ag_copy(c, i).start()
        if z_done <= len(z_steps):
            z_advance(z_done)
            z_done += 1
        c = t - (levels - 1)
        if c >= 0:
            rows = rows_x[:, :, cols(c)].reshape(split * block, chunk)
            gate = gate + jnp.dot(rows, wg[cols(c), :], preferred_element_type=F32)
            upper = upper + jnp.dot(rows, wu[cols(c), :], preferred_element_type=F32)
    hidden = (gate / (1.0 + jnp.exp(-gate)) * upper).astype(BF16)

    local[4].wait()
    for c in range(chunks):
        part = jnp.dot(hidden, wd[:, cols(c)], preferred_element_type=F32)
        for j in range(split):
            piece = part[j * block:(j + 1) * block]
            if trees[c].height[j] == 0:
                send_y[j, :, cols(c)] = piece.astype(BF16)
                rs_copy(c, j).start()
            else:
                part_y[j, :, cols(c)] = piece

    while z_done <= len(z_steps):
        z_advance(z_done)
        z_done += 1
    z_ref[...] = z_acc[len(z_steps)][0:1, 0:1] / tokens_all

    def mix(c, rows_of):
        mixed = weights[0] * jnp.dot(places[0], rows_of(0), preferred_element_type=F32)
        for k in range(1, groups):
            mixed = mixed + weights[k] * jnp.dot(places[k], rows_of(k), preferred_element_type=F32)
        out_ref[:, cols(c)] = mixed.astype(out_ref.dtype)

    tallest = trees[0].height[0]
    for t in range(chunks + tallest - 1):
        for height in range(tallest, 0, -1):
            c = t - (height - 1)
            if not 0 <= c < chunks:
                continue
            for j in range(split):
                if trees[c].height[j] != height:
                    continue
                total = part_y[j, :, cols(c)]
                for i in reversed(trees[c].children[j]):
                    rs_copy(c, i).wait_recv()
                    total = total + recv_y[i, :, cols(c)].astype(F32)
                if j:
                    send_y[j, :, cols(c)] = total.astype(BF16)
                    rs_copy(c, j).start()
                elif groups == 1:
                    done = total.astype(BF16)
                    mix(c, lambda k: done)
                else:
                    send_y[0, :, cols(c)] = total.astype(BF16)

    if groups > 1:
        for k in range(groups):
            for c in range(chunks):
                piece = jnp.dot(collect(k), send_y[0, :, cols(c)], preferred_element_type=F32).astype(BF16)
                back_out[k, :, cols(c)] = piece
            if k:
                across(k, back_out, back_in, bk_send, bk_recv).start()
        for k in range(1, groups):
            across(k, back_out, back_in, bk_send, bk_recv).wait()
        for c in range(chunks):
            mix(c, lambda k: (back_in if k else back_out)[k, :, cols(c)])

    for c in range(chunks):
        for j in range(1, split):
            ag_copy(c, j).wait_send()
            rs_copy(c, j).wait_send()


def body(ex_size, dp_size, tokens, router_weight, chosen, w_gate, w_up, w_down):
    token_rows, picked = tokens[0], chosen[0]
    groups, cap = picked.shape
    rows_dev, width = token_rows.shape
    split = ex_size // groups
    levels = split.bit_length() - 1
    most = 2 * cap // ex_size
    block = groups * most
    ex_bits = ex_size.bit_length() - 1
    dp_bits = dp_size.bit_length() - 1
    chunks = max(1, width // 512)
    chunk = width // chunks
    plain = tuple(range(levels - 1, -1, -1))
    swapped = plain[:-2] + plain[:-3:-1]
    trees = [Tree(levels, swapped if c % 4 == 1 else plain) for c in range(chunks)]
    cfg = (groups, split, most, dp_bits, ex_bits, trees, chunk, float(dp_size * ex_size * rows_dev))
    z_slots = ex_bits + dp_bits + 1
    hidden = w_gate.shape[1]
    dma = pltpu.SemaphoreType.DMA
    scratch = [
        pltpu.VMEM((rows_dev, width), BF16),
        pltpu.VMEM(router_weight.shape, BF16),
        pltpu.VMEM((width, hidden), BF16),
        pltpu.VMEM((width, hidden), BF16),
        pltpu.VMEM((hidden, width), BF16),
        pltpu.VMEM((split, block, width), BF16),
        pltpu.VMEM((split, block, width), BF16),
        pltpu.VMEM((split, block, width), BF16),
        pltpu.VMEM((split, block, width), F32),
        pltpu.VMEM((z_slots, 8, 128), F32),
        pltpu.VMEM((z_slots, 8, 128), F32),
        dma((5,)),
        dma((chunks, split)),
        dma((chunks, split)),
        dma((chunks, split)),
        dma((chunks, split)),
        dma((z_slots,)),
        dma((z_slots,)),
    ]
    if groups > 1:
        scratch += [pltpu.VMEM((groups, most, width), BF16)] * 4 + [dma((groups,))] * 4
    any_spec = pl.BlockSpec(memory_space=pl.ANY)
    vmem_spec = pl.BlockSpec(memory_space=pltpu.VMEM)
    combined, z_loss = pl.pallas_call(
        functools.partial(kernel, cfg),
        out_shape=(
            jax.ShapeDtypeStruct((rows_dev, width), BF16),
            jax.ShapeDtypeStruct((1, 1), F32),
        ),
        in_specs=[any_spec, any_spec, vmem_spec, any_spec, any_spec, any_spec],
        out_specs=(vmem_spec, vmem_spec),
        scratch_shapes=scratch,
        compiler_params=pltpu.CompilerParams(collective_id=0, has_side_effects=True),
    )(token_rows, router_weight, picked, w_gate, w_up, w_down)
    return combined[None], z_loss.reshape(())


def solution(mesh):
    in_specs = (
        P("dp", "expert", None),
        P(),
        P("dp", None, None),
        P(None, "expert"),
        P(None, "expert"),
        P("expert", None),
    )
    out_specs = (P("dp", "expert", None), P())
    step = functools.partial(body, mesh.shape["expert"], mesh.shape["dp"])
    return jax.shard_map(step, mesh=mesh, in_specs=in_specs, out_specs=out_specs, check_vma=False)
```

time: 233 us -> 104 us (0.45)
  waiting for transfers between devices: 136 us -> 0 us
  Pallas kernels: 0 us -> 92.2 us
  blocking collectives: 41.2 us -> 0 us
  other arithmetic: 20 us -> 0 us
  starting transfers between devices: 17.7 us -> 0 us
  matrix products: 8.87 us -> 0 us
  local copies, waits for them, and re-layouts: 6.09 us -> 8.71 us
    pallas_call x0 -> x1, Pallas kernels: none -> 92.2 us  [body(): pl.pallas_call(functools.partial(kernel, cfg), out_shape=(jax.ShapeDtypeS...]
    ppermute x3 -> x0, waiting for transfers between devices: 87.7 us -> none  [partner(): return lax.ppermute(value, axis, pairs)]
    all_to_all x2 -> x0, waiting for transfers between devices: 48.3 us -> none  [the longest x1 48.3 us: body(): lax.all_to_all(outgoing, 'expert', split_axis=0, concat_axis=0, tiled=True)]
    psum x1 -> x0, blocking collectives: 41.2 us -> none  [body(): loss_total = lax.psum(jnp.sum(log_total * log_total), ('dp', 'expert'))]
    all_to_all x2 -> x0, starting transfers between devices: 12.2 us -> none  [the longest x1 7.28 us: body(): lax.all_to_all(outgoing, 'expert', split_axis=0, concat_axis=0, tiled=True)]
    dot_general x3 -> x0, matrix products: 8.87 us -> none  [the longest x1 5.43 us: body(): jnp.dot(hidden, w_down, preferred_element_type=jnp.float32)]
    select_n x6 -> x0, other arithmetic: 8.69 us -> none  [the longest x2 6.07 us: body(): keeping = jnp.where(lower_side, lower_half, upper_half)]
    unnamed x9 -> x5, local copies, waits for them, and re-layouts: 0.06 us -> 8.71 us
  transfers between devices with their start and end apart: 5 -> 0, of which waited for: 4 -> 0; matrix products, arithmetic and copies ran while one was open for 1% -> 0% of each run, Pallas kernels for 0% -> 0%
where the time goes in v1:
time: 104 us; the launch traced here: 103 us
  Pallas kernels  92.2 us (89%)
  local copies, waits for them, and re-layouts  8.71 us (8%)
  between operations  2.47 us (2%)
    pallas_call x1, Pallas kernels, body(): pl.pallas_call(functools.partial(kernel, cfg), out_shape=(jax.ShapeDtypeS...  92.2 us
    unnamed x5, local copies, waits for them, and re-layouts  8.71 us

profile of v1, /device:TPU:0, one launch (start us, length us, event | category | flops | bytes accessed | tf_op | source)
XLA Modules:
  0.0 103.4 jit_solution(10422871667676168761)
XLA Ops:
  0.6 0.0 copy-start
  0.6 4.0 %copy.8.refs_3_ = bf16[4096,192]{1,0:T(8,128)(2,1)} copy(bf16[4096,192]{0,1:T(8,128)(2,1)} %param.9) | data formatting | bytes 3145728 | tf_op args[3]
  4.6 0.0 copy-done
  4.6 2.4 %copy.9.refs_4_ = bf16[4096,192]{1,0:T(8,128)(2,1)} copy(bf16[4096,192]{0,1:T(8,128)(2,1)S(1)} %copy-done) | data formatting | bytes 3145728 | tf_op args[4]
  7.1 92.2 %shard_map.77 = (bf16[128,4096]{1,0:T(8,128)(2,1)}, f32[1,1]{1,0:T(1,128)}) custom-call(bf16[128,4096]{1,0:T(8,128)(2,1)} %bitcast.4, bf16[4096,128]{1,0:T(8,128)(2,1)} %refs_1_.1, s32[1,128]{1,0:T(1,128)} %bitcast.6, bf16[4096,192]{1,0:T(8,128)(2,1)} %copy.8.refs_3_, bf16[4096,192]{1,0:T(8,128)(2,1)} %copy.9.refs_4_, bf16[192,4096]{1,0:T(8,128)(2,1)} %refs_5_.1), custom_call_target="tpu_custom_call" | custom-call | tf_op jit(solution)/shard_map/pallas_call | solution.py:337
  99.3 2.3 %copy.12 = bf16[1,128,4096]{2,1,0:T(8,128)(2,1)} copy(bf16[1,128,4096]{2,1,0:T(8,128)(2,1)} %bitcast.5) | data formatting | bytes 2097152
Async XLA Ops:
  0.6 4.0 %copy-start = (bf16[4096,192]{0,1:T(8,128)(2,1)S(1)}, bf16[4096,192]{0,1:T(8,128)(2,1)}, u32[]{:S(2)}) copy-start(bf16[4096,192]{0,1:T(8,128)(2,1)} %param.10) | copy-start | bytes 4718596

commit v2 on v1

--- a/solution.py
+++ b/solution.py
@@ -10,6 +10,7 @@
 MESH = pl.DeviceIdType.MESH
 F32 = jnp.float32
 BF16 = jnp.bfloat16
+LAG = 1
 
 
 def flip(index, mask):
@@ -22,37 +23,25 @@
     return result
 
 
-class Tree:
-    def __init__(self, levels, order):
-        self.blocks = 2**levels
-        self.bit = {}
-        for j in range(1, self.blocks):
-            self.bit[j] = [b for b in order if j >> b & 1][-1]
-        self.parent = {j: j ^ 1 << b for j, b in self.bit.items()}
-        self.children = [
-            sorted((j for j in self.parent if self.parent[j] == i), key=lambda j: order.index(self.bit[j]))
-            for i in range(self.blocks)
-        ]
-        self.depth = [bin(j).count("1") for j in range(self.blocks)]
-        self.height = [self._height(j) for j in range(self.blocks)]
-
-    def _height(self, j):
-        return 1 + max(self._height(i) for i in self.children[j]) if self.children[j] else 0
+def times_t(a, b):
+    return lax.dot_general(a, b, (((1,), (1,)), ((), ())), preferred_element_type=F32)
+
+
+def source(j):
+    return j - 1 if j % 2 else 0
 
 
 def kernel(cfg, *refs):
-    groups, split, most, dp_bits, ex_bits, trees, chunk, tokens_all = cfg
+    groups, split, most, dp_bits, ex_bits, chunks, chunk, tokens_all = cfg
     (tok_h, rw_h, chosen_ref, wg_h, wu_h, wd_h, out_ref, z_ref,
      tok, rw, wg, wu, wd, rows_x, send_y, recv_y, part_y, z_acc, z_in,
      local_sem, ag_send, ag_recv, rs_send, rs_recv, z_send, z_recv) = refs[:26]
-    levels = split.bit_length() - 1
     me = lax.axis_index("expert")
     me_dp = lax.axis_index("dp")
     my_group = me // split
     rows_dev, width = tok.shape
     cap = chosen_ref.shape[1]
     block = groups * most
-    chunks = len(trees)
 
     local = [
         pltpu.make_async_copy(src, dst, local_sem.at[i])
@@ -61,7 +50,7 @@
     for copy in local:
         copy.start()
 
-    ex_masks = [1 << b for b in range(levels)] + [split * k for k in range(1, groups)]
+    ex_masks = [1] + list(range(2, split, 2)) + [split * k for k in range(1, groups)]
     partners = [{"expert": flip(me, mask)} for mask in ex_masks]
     partners += [{"dp": flip(me_dp, 1 << b)} for b in range(dp_bits)]
     barrier = pltpu.get_barrier_semaphore()
@@ -81,7 +70,7 @@
         equal = (row == t_sub).astype(F32)
         member = jnp.max(equal, axis=1, keepdims=True)
         ones = jnp.ones((8, cap), BF16)
-        member_row = lax.dot_general(ones, equal.astype(BF16), (((1,), (1,)), ((), ())), preferred_element_type=F32)
+        member_row = times_t(ones, equal.astype(BF16))
         rank_row = jnp.dot(member_row.astype(BF16), before, preferred_element_type=F32)
         pick = jnp.where(member_row[0:1] > 0.5, (rank_row[0:1] == slot_sub).astype(F32), 0.0)
         wide = jnp.broadcast_to(member, (rows_dev, most))
@@ -95,26 +84,26 @@
         return pl.ds(c * chunk, chunk)
 
     def ag_copy(c, j):
-        tree = trees[c]
         return pltpu.make_async_remote_copy(
-            src_ref=rows_x.at[tree.parent[j], :, cols(c)],
-            dst_ref=rows_x.at[j, :, cols(c)],
+            src_ref=rows_x.at[c, source(j)],
+            dst_ref=rows_x.at[c, j],
             send_sem=ag_send.at[c, j],
             recv_sem=ag_recv.at[c, j],
-            device_id={"expert": flip(me, 1 << tree.bit[j])},
+            device_id={"expert": flip(me, j - source(j))},
             device_id_type=MESH,
         )
 
     def rs_copy(c, j):
-        tree = trees[c]
         return pltpu.make_async_remote_copy(
-            src_ref=send_y.at[j, :, cols(c)],
-            dst_ref=recv_y.at[j, :, cols(c)],
+            src_ref=send_y.at[c, j],
+            dst_ref=recv_y.at[c, j],
             send_sem=rs_send.at[c, j],
             recv_sem=rs_recv.at[c, j],
-            device_id={"expert": flip(me, 1 << tree.bit[j])},
+            device_id={"expert": flip(me, j - source(j))},
             device_id_type=MESH,
         )
+
+    far = [j for j in range(split - 2, 0, -2)]
 
     z_steps = [("expert", flip(me, 1 << b)) for b in range(ex_bits)]
     z_steps += [("dp", flip(me_dp, 1 << b)) for b in range(dp_bits)]
@@ -141,8 +130,8 @@
     local[0].wait()
     if groups == 1:
         for c in range(chunks):
-            rows_x[0, :, cols(c)] = jnp.dot(picks[0], tok[:, cols(c)], preferred_element_type=F32).astype(BF16)
-            for j in trees[c].children[0]:
+            rows_x[c, 0] = jnp.dot(picks[0], tok[:, cols(c)], preferred_element_type=F32).astype(BF16)
+            for j in far + [1]:
                 ag_copy(c, j).start()
     else:
         slots, stage, back_out, back_in, ex_send, ex_recv, bk_send, bk_recv = refs[26:]
@@ -178,8 +167,8 @@
             total = jnp.dot(spread(0), slots[0, :, cols(c)], preferred_element_type=F32)
             for k in range(1, groups):
                 total = total + jnp.dot(spread(k), stage[k, :, cols(c)], preferred_element_type=F32)
-            rows_x[0, :, cols(c)] = total.astype(BF16)
-            for j in trees[c].children[0]:
+            rows_x[c, 0] = total.astype(BF16)
+            for j in far + [1]:
                 ag_copy(c, j).start()
 
     local[3].wait()
@@ -207,38 +196,40 @@
 
     local[1].wait()
     local[2].wait()
-    gate = jnp.zeros((split * block, wg.shape[1]), F32)
-    upper = jnp.zeros((split * block, wg.shape[1]), F32)
+    gate = jnp.zeros((split * block, wg.shape[0]), F32)
+    upper = jnp.zeros((split * block, wg.shape[0]), F32)
     z_done = 0
-    for t in range(chunks + levels - 1):
-        for depth in range(levels, 0, -1):
-            c = t - (depth - 1)
-            if 0 <= c < chunks:
-                for j in range(split):
-                    if trees[c].depth[j] == depth:
-                        ag_copy(c, j).wait_recv()
-                        for i in trees[c].children[j]:
-                            ag_copy(c, i).start()
+    for t in range(chunks + LAG):
+        if t < chunks:
+            for j in reversed(far):
+                ag_copy(t, j).wait_recv()
+                ag_copy(t, j + 1).start()
         if z_done <= len(z_steps):
             z_advance(z_done)
             z_done += 1
-        c = t - (levels - 1)
+        c = t - LAG
         if c >= 0:
-            rows = rows_x[:, :, cols(c)].reshape(split * block, chunk)
-            gate = gate + jnp.dot(rows, wg[cols(c), :], preferred_element_type=F32)
-            upper = upper + jnp.dot(rows, wu[cols(c), :], preferred_element_type=F32)
+            for j in range(1, split, 2):
+                ag_copy(c, j).wait_recv()
+            rows = rows_x[c].reshape(split * block, chunk)
+            gate = gate + times_t(rows, wg[:, cols(c)])
+            upper = upper + times_t(rows, wu[:, cols(c)])
     hidden = (gate / (1.0 + jnp.exp(-gate)) * upper).astype(BF16)
 
     local[4].wait()
-    for c in range(chunks):
+
+    def down(c):
         part = jnp.dot(hidden, wd[:, cols(c)], preferred_element_type=F32)
-        for j in range(split):
+        for j in reversed(range(split)):
             piece = part[j * block:(j + 1) * block]
-            if trees[c].height[j] == 0:
-                send_y[j, :, cols(c)] = piece.astype(BF16)
+            if j % 2:
+                send_y[c, j] = piece.astype(BF16)
                 rs_copy(c, j).start()
             else:
-                part_y[j, :, cols(c)] = piece
+                part_y[c, j // 2] = piece
+
+    for c in range(chunks):
+        down(c)
 
     while z_done <= len(z_steps):
         z_advance(z_done)
@@ -251,32 +242,28 @@
             mixed = mixed + weights[k] * jnp.dot(places[k], rows_of(k), preferred_element_type=F32)
         out_ref[:, cols(c)] = mixed.astype(out_ref.dtype)
 
-    tallest = trees[0].height[0]
-    for t in range(chunks + tallest - 1):
-        for height in range(tallest, 0, -1):
-            c = t - (height - 1)
-            if not 0 <= c < chunks:
-                continue
-            for j in range(split):
-                if trees[c].height[j] != height:
-                    continue
-                total = part_y[j, :, cols(c)]
-                for i in reversed(trees[c].children[j]):
-                    rs_copy(c, i).wait_recv()
-                    total = total + recv_y[i, :, cols(c)].astype(F32)
-                if j:
-                    send_y[j, :, cols(c)] = total.astype(BF16)
-                    rs_copy(c, j).start()
-                elif groups == 1:
-                    done = total.astype(BF16)
-                    mix(c, lambda k: done)
-                else:
-                    send_y[0, :, cols(c)] = total.astype(BF16)
+    for t in range(chunks + LAG):
+        if t < chunks:
+            for j in far:
+                rs_copy(t, j + 1).wait_recv()
+                send_y[t, j] = (part_y[t, j // 2] + recv_y[t, j + 1].astype(F32)).astype(BF16)
+                rs_copy(t, j).start()
+        c = t - LAG
+        if c >= 0:
+            total = part_y[c, 0]
+            for j in [1] + far:
+                rs_copy(c, j).wait_recv()
+                total = total + recv_y[c, j].astype(F32)
+            done = total.astype(BF16)
+            if groups == 1:
+                mix(c, lambda k: done)
+            else:
+                send_y[c, 0] = done
 
     if groups > 1:
         for k in range(groups):
             for c in range(chunks):
-                piece = jnp.dot(collect(k), send_y[0, :, cols(c)], preferred_element_type=F32).astype(BF16)
+                piece = jnp.dot(collect(k), send_y[c, 0], preferred_element_type=F32).astype(BF16)
                 back_out[k, :, cols(c)] = piece
             if k:
                 across(k, back_out, back_in, bk_send, bk_recv).start()
@@ -296,30 +283,26 @@
     groups, cap = picked.shape
     rows_dev, width = token_rows.shape
     split = ex_size // groups
-    levels = split.bit_length() - 1
     most = 2 * cap // ex_size
     block = groups * most
     ex_bits = ex_size.bit_length() - 1
     dp_bits = dp_size.bit_length() - 1
-    chunks = max(1, width // 512)
+    chunks = max(1, width // 1024)
     chunk = width // chunks
-    plain = tuple(range(levels - 1, -1, -1))
-    swapped = plain[:-2] + plain[:-3:-1]
-    trees = [Tree(levels, swapped if c % 4 == 1 else plain) for c in range(chunks)]
-    cfg = (groups, split, most, dp_bits, ex_bits, trees, chunk, float(dp_size * ex_size * rows_dev))
+    cfg = (groups, split, most, dp_bits, ex_bits, chunks, chunk, float(dp_size * ex_size * rows_dev))
     z_slots = ex_bits + dp_bits + 1
     hidden = w_gate.shape[1]
     dma = pltpu.SemaphoreType.DMA
     scratch = [
         pltpu.VMEM((rows_dev, width), BF16),
         pltpu.VMEM(router_weight.shape, BF16),
-        pltpu.VMEM((width, hidden), BF16),
-        pltpu.VMEM((width, hidden), BF16),
         pltpu.VMEM((hidden, width), BF16),
-        pltpu.VMEM((split, block, width), BF16),
-        pltpu.VMEM((split, block, width), BF16),
-        pltpu.VMEM((split, block, width), BF16),
-        pltpu.VMEM((split, block, width), F32),
+        pltpu.VMEM((hidden, width), BF16),
+        pltpu.VMEM((hidden, width), BF16),
+        pltpu.VMEM((chunks, split, block, chunk), BF16),
+        pltpu.VMEM((chunks, split, block, chunk), BF16),
+        pltpu.VMEM((chunks, split, block, chunk), BF16),
+        pltpu.VMEM((chunks, split // 2, block, chunk), F32),
         pltpu.VMEM((z_slots, 8, 128), F32),
         pltpu.VMEM((z_slots, 8, 128), F32),
         dma((5,)),
@@ -344,7 +327,7 @@
         out_specs=(vmem_spec, vmem_spec),
         scratch_shapes=scratch,
         compiler_params=pltpu.CompilerParams(collective_id=0, has_side_effects=True),
-    )(token_rows, router_weight, picked, w_gate, w_up, w_down)
+    )(token_rows, router_weight, picked, w_gate.T, w_up.T, w_down)
     return combined[None], z_loss.reshape(())
 
 

time: 104 us -> 69.3 us (0.67)
  Pallas kernels: 92.2 us -> 64.5 us
  local copies, waits for them, and re-layouts: 8.71 us -> 2.29 us
    pallas_call x1, Pallas kernels: 92.2 us -> 64.5 us  [body(): pl.pallas_call(functools.partial(kernel, cfg), out_shape=(jax.ShapeDtypeS...]
    unnamed x5 -> x1, local copies, waits for them, and re-layouts: 8.71 us -> 2.29 us
where the time goes in v2:
time: 69.3 us; the launch traced here: 69.1 us
  Pallas kernels  64.5 us (93%)
  between operations  2.33 us (3%)
  local copies, waits for them, and re-layouts  2.29 us (3%)
    pallas_call x1, Pallas kernels, body(): pl.pallas_call(functools.partial(kernel, cfg), out_shape=(jax.ShapeDtypeS...  64.5 us
    unnamed x1, local copies, waits for them, and re-layouts  2.29 us

profile of v2, /device:TPU:0, one launch (start us, length us, event | category | flops | bytes accessed | tf_op | source)
XLA Modules:
  0.0 69.1 jit_solution(11310592873298951927)
XLA Ops:
  0.6 64.5 %shard_map.77 = (bf16[128,4096]{1,0:T(8,128)(2,1)}, f32[1,1]{1,0:T(1,128)}) custom-call(bf16[128,4096]{1,0:T(8,128)(2,1)} %bitcast.9, bf16[4096,128]{1,0:T(8,128)(2,1)} %refs_1_.1, s32[1,128]{1,0:T(1,128)} %bitcast.10, bf16[192,4096]{1,0:T(8,128)(2,1)} %bitcast.6, bf16[192,4096]{1,0:T(8,128)(2,1)} %bitcast.7, bf16[192,4096]{1,0:T(8,128)(2,1)} %refs_5_.1), custom_call_target="tpu_custom_call" | custom-call | tf_op jit(solution)/shard_map/pallas_call | solution.py:320
  65.2 2.3 %copy.10 = bf16[1,128,4096]{2,1,0:T(8,128)(2,1)} copy(bf16[1,128,4096]{2,1,0:T(8,128)(2,1)} %bitcast.8) | data formatting | bytes 2097152

commit v3 on v2

--- a/solution.py
+++ b/solution.py
@@ -35,7 +35,7 @@
     groups, split, most, dp_bits, ex_bits, chunks, chunk, tokens_all = cfg
     (tok_h, rw_h, chosen_ref, wg_h, wu_h, wd_h, out_ref, z_ref,
      tok, rw, wg, wu, wd, rows_x, send_y, recv_y, part_y, z_acc, z_in,
-     local_sem, ag_send, ag_recv, rs_send, rs_recv, z_send, z_recv) = refs[:26]
+     local_sem, out_v, out_sem, ag_send, ag_recv, rs_send, rs_recv, z_send, z_recv) = refs[:28]
     me = lax.axis_index("expert")
     me_dp = lax.axis_index("dp")
     my_group = me // split
@@ -131,10 +131,12 @@
     if groups == 1:
         for c in range(chunks):
             rows_x[c, 0] = jnp.dot(picks[0], tok[:, cols(c)], preferred_element_type=F32).astype(BF16)
-            for j in far + [1]:
+            for j in far:
                 ag_copy(c, j).start()
+        for c in range(chunks):
+            ag_copy(c, 1).start()
     else:
-        slots, stage, back_out, back_in, ex_send, ex_recv, bk_send, bk_recv = refs[26:]
+        slots, stage, back_out, back_in, ex_send, ex_recv, bk_send, bk_recv = refs[28:]
 
         def across(k, src, dst, send, recv):
             return pltpu.make_async_remote_copy(
@@ -236,11 +238,15 @@
         z_done += 1
     z_ref[...] = z_acc[len(z_steps)][0:1, 0:1] / tokens_all
 
+    def out_copy(c):
+        return pltpu.make_async_copy(out_v.at[:, cols(c)], out_ref.at[:, cols(c)], out_sem.at[c])
+
     def mix(c, rows_of):
         mixed = weights[0] * jnp.dot(places[0], rows_of(0), preferred_element_type=F32)
         for k in range(1, groups):
             mixed = mixed + weights[k] * jnp.dot(places[k], rows_of(k), preferred_element_type=F32)
-        out_ref[:, cols(c)] = mixed.astype(out_ref.dtype)
+        out_v[:, cols(c)] = mixed.astype(out_v.dtype)
+        out_copy(c).start()
 
     for t in range(chunks + LAG):
         if t < chunks:
@@ -276,6 +282,7 @@
         for j in range(1, split):
             ag_copy(c, j).wait_send()
             rs_copy(c, j).wait_send()
+        out_copy(c).wait()
 
 
 def body(ex_size, dp_size, tokens, router_weight, chosen, w_gate, w_up, w_down):
@@ -306,6 +313,8 @@
         pltpu.VMEM((z_slots, 8, 128), F32),
         pltpu.VMEM((z_slots, 8, 128), F32),
         dma((5,)),
+        pltpu.VMEM((rows_dev, width), BF16),
+        dma((chunks,)),
         dma((chunks, split)),
         dma((chunks, split)),
         dma((chunks, split)),
@@ -324,7 +333,7 @@
             jax.ShapeDtypeStruct((1, 1), F32),
         ),
         in_specs=[any_spec, any_spec, vmem_spec, any_spec, any_spec, any_spec],
-        out_specs=(vmem_spec, vmem_spec),
+        out_specs=(any_spec, vmem_spec),
         scratch_shapes=scratch,
         compiler_params=pltpu.CompilerParams(collective_id=0, has_side_effects=True),
     )(token_rows, router_weight, picked, w_gate.T, w_up.T, w_down)

time: 69.3 us -> 69.5 us (level)
  no operation moved by 1% of the time
where the time goes in v3:
time: 69.5 us; the launch traced here: 69.3 us
  Pallas kernels  64.7 us (93%)
  between operations  2.33 us (3%)
  local copies, waits for them, and re-layouts  2.29 us (3%)
    pallas_call x1, Pallas kernels, body(): pl.pallas_call(functools.partial(kernel, cfg), out_shape=(jax.ShapeDtypeS...  64.7 us
    unnamed x1, local copies, waits for them, and re-layouts  2.29 us

profile of v3, /device:TPU:0, one launch (start us, length us, event | category | flops | bytes accessed | tf_op | source)
XLA Modules:
  0.0 69.3 jit_solution(17584691808725800287)
XLA Ops:
  0.6 64.7 %shard_map.77 = (bf16[128,4096]{1,0:T(8,128)(2,1)}, f32[1,1]{1,0:T(1,128)}) custom-call(bf16[128,4096]{1,0:T(8,128)(2,1)} %bitcast.9, bf16[4096,128]{1,0:T(8,128)(2,1)} %refs_1_.1, s32[1,128]{1,0:T(1,128)} %bitcast.10, bf16[192,4096]{1,0:T(8,128)(2,1)} %bitcast.6, bf16[192,4096]{1,0:T(8,128)(2,1)} %bitcast.7, bf16[192,4096]{1,0:T(8,128)(2,1)} %refs_5_.1), custom_call_target="tpu_custom_call" | custom-call | tf_op jit(solution)/shard_map/pallas_call | solution.py:329
  65.3 2.3 %copy.10 = bf16[1,128,4096]{2,1,0:T(8,128)(2,1)} copy(bf16[1,128,4096]{2,1,0:T(8,128)(2,1)} %bitcast.8) | data formatting | bytes 2097152
